TPU v7x, 32 devices: a whole 2x2x4 slice. The times are simulated.
32 devices in a mesh: row: 4 (over z), col: 8 (over y, x, core).
Axes of the slice: x: 2, y: 2, z: 4, core: 2. Of those that a mesh axis runs over, the one named last changes fastest.
Arguments:
- inverse_block: float32 [512, 512], P('row', 'col'), as said below
- panels: bfloat16 [2, 512, 512], P(None, 'row'), may hold values from -0.375 to 0.375
- pattern: int32 [2, 4], replicated, may hold values 0 or 1
Outputs:
- inverse_panel: float32 [2, 512, 512], P(None, ('row', 'col'))
- update: float32 [2, 512, 512], P(None, 'col')
Inputs may be any that keep to these rules, and one draw needn't show every extreme that they name: `pattern`: 1 marks a block of rows in the supernode's structure, 0 a block outside it. `inverse_block`: symmetric.
All inputs are finite; a program needn't handle non-finite values.
Results may differ from a plain program's by a relative error of at most 0.00045.
Values may be sent and summed in bfloat16 or wider, within the bound.
No kernel may reach another device: no remote copies, remote signals or barrier semaphores. Data moves between devices by JAX's collectives and lax.ppermute only.
A program may use at most 64 MiB of HBM per device.

v0:
```python
import jax
import jax.numpy as jnp
from jax import lax
from jax.sharding import PartitionSpec as P

BLOCK = 128


def spread(block, axis, source):
    block = jnp.where(lax.axis_index(axis) == source, block, jnp.zeros_like(block))
    return lax.psum(block, axis)


def shards(inverse_block, panels, pattern):
    row_count = lax.axis_size("row")
    col_count = lax.axis_size("col")
    row_index = lax.axis_index("row")
    col_index = lax.axis_index("col")
    rows_here = panels.shape[1]
    cols_here = inverse_block.shape[1]
    ratio = col_count // row_count
    span = rows_here // col_count
    width = panels.shape[2]
    blocks = pattern.shape[1]
    row_ids = row_index * rows_here + jnp.arange(rows_here, dtype=jnp.int32)
    onehot = (row_ids // BLOCK)[:, None] == jnp.arange(blocks, dtype=jnp.int32)[None, :]
    row_mask = jnp.sum(jnp.where(onehot[None, :, :], pattern[:, None, :], 0), axis=2)
    used = panels * row_mask[:, :, None].astype(jnp.bfloat16)
    piece = lax.dynamic_slice_in_dim(used, col_index % ratio * cols_here, cols_here, 1)
    col_panel = spread(piece, "row", col_index // ratio)
    product = jnp.einsum(
        "ij,sjw->siw", inverse_block, col_panel.astype(jnp.float32), precision=lax.Precision.HIGHEST
    )
    term = -(product * row_mask[:, :, None].astype(jnp.float32))
    share = width // col_count
    partial_update = jnp.einsum(
        "siv,siw->svw", used.astype(jnp.float32), term, precision=lax.Precision.HIGHEST
    )
    panel_parts = term.reshape(2, col_count, span, width)
    update_parts = partial_update.reshape(2, col_count, share, width)
    joined = jnp.concatenate([panel_parts, update_parts], axis=2).reshape(
        2, col_count * (span + share), width
    )
    received = lax.psum_scatter(joined, "col", scatter_dimension=1, tiled=True)
    inverse_panel = received[:, :span]
    update = -lax.psum(received[:, span:], "row")
    return (inverse_panel, update)


def solution(mesh):
    return jax.shard_map(
        shards,
        mesh=mesh,
        in_specs=(P("row", "col"), P(None, "row", None), P()),
        out_specs=(P(None, ("row", "col"), None), P(None, "col", None)),
        check_vma=False,
    )
```

profile of v0, /device:TPU:0, one launch (start us, length us, event | category | flops | bytes accessed | tf_op | source)
XLA Modules:
  0.0 142.5 jit_solution(808378041422368606)
XLA Ops:
  7.2 0.0 copy-start
  7.2 0.0 all-reduce.3.cloned.1.call-start
  7.3 0.8 select_reduce_fusion
  8.1 1.1 broadcast_multiply_fusion
  9.1 0.7 dynamic-slice_select_fusion
  9.8 0.0 all-reduce.3.cloned.1.call-update
  9.8 0.0 reduce-scatter.2.cloned.1.call-start
  9.9 38.4 %all-reduce.3.cloned.1.call-done = bf16[2,64,512]{2,1,0:T(8,128)(2,1)} async-done(((bf16[2,64,512]{2,1,0:T(8,128)(2,1)}), bf16[2,64,512]{2,1,0:T(8,128)(2,1)}) %all-reduce.3.cloned.1.call-update) | async-done | bytes 131088 | tf_op jit(solution)/shard_map/psum | solution.py:11
  48.3 0.0 copy-done
  48.3 1.3 fusion
  49.6 1.0 fusion.3
  50.7 1.7 %pad_maximum_fusion = f32[2,8,80,512]{3,2,1,0:T(8,128)} fusion(f32[2,8,64,512]{3,2,1,0:T(8,128)S(1)} %bitcast.12, f32[2,8,16,512]{3,2,1,0:T(8,128)S(1)} %bitcast.13), kind=kLoop, calls=%fused_computation | loop fusion | flops 655360 | bytes 5242880 | tf_op jit(solution)/shard_map/concatenate | solution.py:41
  52.4 0.0 reduce-scatter.2.cloned.1.call-update
  52.4 0.0 all-reduce.5.cloned.1.call-start
  52.5 43.3 %reduce-scatter.2.cloned.1.call-done = f32[2,80,512]{2,1,0:T(8,128)} async-done(((f32[2,640,512]{2,1,0:T(8,128)}), f32[2,80,512]{2,1,0:T(8,128)}) %reduce-scatter.2.cloned.1.call-update) | async-done | bytes 327696 | tf_op jit(solution)/shard_map/reduce_scatter | solution.py:44
  95.8 1.7 %slice.9 = f32[2,64,512]{2,1,0:T(8,128)} slice(f32[2,80,512]{2,1,0:T(8,128)} %reduce-scatter.2.cloned.1.call-done), slice={[0:2], [16:80], [0:512]} | slice | bytes 524288 | tf_op jit(solution)/shard_map/slice | solution.py:46
  97.4 0.0 all-reduce.5.cloned.1.call-update
  97.5 1.5 %slice.8 = f32[2,16,512]{2,1,0:T(8,128)} slice(f32[2,80,512]{2,1,0:T(8,128)} %reduce-scatter.2.cloned.1.call-done), slice={[0:2], [0:16], [0:512]} | slice | bytes 131072 | tf_op jit(solution)/shard_map/slice | solution.py:45
  98.9 35.4 %all-reduce.5.cloned.1.call-done = f32[2,64,512]{2,1,0:T(8,128)} async-done(((f32[2,64,512]{2,1,0:T(8,128)}), f32[2,64,512]{2,1,0:T(8,128)}) %all-reduce.5.cloned.1.call-update) | async-done | bytes 262160 | tf_op jit(solution)/shard_map/psum | solution.py:46
  134.3 1.7 %neg.11 = f32[2,64,512]{2,1,0:T(8,128)} negate(f32[2,64,512]{2,1,0:T(8,128)} %all-reduce.5.cloned.1.call-done) | non-fusion elementwise | flops 65536 | bytes 524288 | tf_op jit(solution)/shard_map/neg | solution.py:46
  (3 shorter events, 0.0 us)
Async XLA Ops:
  7.2 41.1 %copy-start = (f32[128,64]{0,1:T(8,128)S(1)}, f32[128,64]{0,1:T(8,128)}, u32[]{:S(2)}) copy-start(f32[128,64]{0,1:T(8,128)} %param.3) | copy-start | bytes 98308
  7.2 41.1 %all-reduce.3.cloned.1.call-start = ((), (), s32[]{:S(2)}) async-start(), calls=%async_computation.1 | async-start | bytes 262144 | tf_op jit(solution)/shard_map/psum | solution.py:11
  9.8 85.9 %reduce-scatter.2.cloned.1.call-start = ((), (), s32[]{:S(2)}) async-start(), calls=%async_computation.2 | async-start | bytes 2949120 | tf_op jit(solution)/shard_map/reduce_scatter | solution.py:44
  52.4 81.9 %all-reduce.5.cloned.1.call-start = ((), (), s32[]{:S(2)}) async-start(), calls=%async_computation.3 | async-start | bytes 524288 | tf_op jit(solution)/shard_map/psum | solution.py:46
Sparse Core Ops, SparseCore 0:
  10.9 37.3 all-reduce.2
  52.5 43.1 reduce-scatter.1
  98.7 35.5 all-reduce.4
where the time goes:
time: 143 us; the launch traced here: 142 us
  waiting for transfers between devices  117 us (82%)
  between operations  13.8 us (10%)
  other arithmetic  5.95 us (4%)
  local copies, waits for them, and re-layouts  3.16 us (2%)
  matrix products  2.35 us (2%)
    reduce_scatter x1, waiting for transfers between devices, shards(): received = lax.psum_scatter(joined, 'col', scatter_dimension=1, tiled=True)  43.3 us
    psum x1, waiting for transfers between devices, spread(): return lax.psum(block, axis)  38.4 us
    psum x1, waiting for transfers between devices, shards(): update = -lax.psum(received[:, span:], 'row')  35.4 us
  transfers between devices with their start and end apart: 3, of which 3 were waited for; matrix products, arithmetic and copies ran while one was open for 1% of the time, Pallas kernels for 0%

commit v1 on v0

--- a/solution.py
+++ b/solution.py
@@ -6,9 +6,15 @@
 BLOCK = 128
 
 
+def summed_here(x, name):
+    pieces = lax.all_gather(x, name, axis=0, tiled=False)
+    result = pieces.sum(axis=0)
+    return result
+
+
 def spread(block, axis, source):
     block = jnp.where(lax.axis_index(axis) == source, block, jnp.zeros_like(block))
-    return lax.psum(block, axis)
+    return summed_here(block, axis)
 
 
 def shards(inverse_block, panels, pattern):

time: 143 us -> 123 us (0.86)
  waiting for transfers between devices: 117 us -> 80.8 us
  blocking collectives: 0 us -> 17.4 us
    psum x1 -> x0, waiting for transfers between devices: 38.4 us -> none  [spread(): return lax.psum(block, axis)]
    all_gather x0 -> x1, blocking collectives: none -> 17.4 us  [summed_here(): pieces = lax.all_gather(x, name, axis=0, tiled=False)]
    reduce_scatter x1, waiting for transfers between devices: 43.3 us -> 45.4 us  [shards(): received = lax.psum_scatter(joined, 'col', scatter_dimension=1, tiled=True)]
  transfers between devices with their start and end apart: 3 -> 2, of which waited for: 3 -> 2; matrix products, arithmetic and copies ran while one was open for 1% -> 1% of each run, Pallas kernels for 0% -> 0%
where the time goes in v1:
time: 123 us; the launch traced here: 122 us
  waiting for transfers between devices  80.8 us (66%)
  blocking collectives  17.4 us (14%)
  between operations  14.1 us (11%)
  other arithmetic  5.37 us (4%)
  local copies, waits for them, and re-layouts  3.16 us (3%)
  matrix products  1.45 us (1%)
    reduce_scatter x1, waiting for transfers between devices, shards(): received = lax.psum_scatter(joined, 'col', scatter_dimension=1, tiled=True)  45.4 us
    psum x1, waiting for transfers between devices, shards(): update = -lax.psum(received[:, span:], 'row')  35.4 us
    all_gather x1, blocking collectives, summed_here(): pieces = lax.all_gather(x, name, axis=0, tiled=False)  17.4 us
  transfers between devices with their start and end apart: 2, of which 2 were waited for; matrix products, arithmetic and copies ran while one was open for 1% of the time, Pallas kernels for 0%

profile of v1, /device:TPU:0, one launch (start us, length us, event | category | flops | bytes accessed | tf_op | source)
XLA Modules:
  0.0 122.3 jit_solution(11307707514112741565)
XLA Ops:
  7.2 0.0 copy-start
  7.2 0.0 reduce-scatter.2.cloned.1.call-start
  7.3 0.8 select_reduce_fusion
  8.1 1.0 broadcast_multiply_fusion
  9.2 17.4 %all-gather = bf16[8,64,512]{2,1,0:T(8,128)(2,1)S(1)} all-gather(bf16[2,64,512]{2,1,0:T(8,128)(2,1)S(1)} %dynamic-slice_select_fusion), channel_id=2, replica_groups=mesh['row'=4,'col'=8] {'row'}, dimensions={0}, use_global_device_ids=true | all-gather | bytes 655360 | tf_op jit(solution)/shard_map/all_gather | solution.py:10
  26.5 0.1 reduce_sum.22
  26.6 0.0 copy-done
  26.6 0.4 fusion
  27.0 1.0 fusion.3
  28.1 1.7 %pad_maximum_fusion = f32[2,8,80,512]{3,2,1,0:T(8,128)} fusion(f32[2,8,64,512]{3,2,1,0:T(8,128)S(1)} %bitcast.13, f32[2,8,16,512]{3,2,1,0:T(8,128)S(1)} %bitcast.14), kind=kLoop, calls=%fused_computation | loop fusion | flops 655360 | bytes 5242880 | tf_op jit(solution)/shard_map/concatenate | solution.py:47
  29.8 0.0 reduce-scatter.2.cloned.1.call-update
  29.9 0.0 all-reduce.2.cloned.1.call-start
  29.9 45.4 %reduce-scatter.2.cloned.1.call-done = f32[2,80,512]{2,1,0:T(8,128)} async-done(((f32[2,640,512]{2,1,0:T(8,128)}), f32[2,80,512]{2,1,0:T(8,128)}) %reduce-scatter.2.cloned.1.call-update) | async-done | bytes 327696 | tf_op jit(solution)/shard_map/reduce_scatter | solution.py:50
  75.3 1.7 %slice.9 = f32[2,64,512]{2,1,0:T(8,128)} slice(f32[2,80,512]{2,1,0:T(8,128)} %reduce-scatter.2.cloned.1.call-done), slice={[0:2], [16:80], [0:512]} | slice | bytes 524288 | tf_op jit(solution)/shard_map/slice | solution.py:52
  76.9 0.0 all-reduce.2.cloned.1.call-update
  77.0 1.5 %slice.8 = f32[2,16,512]{2,1,0:T(8,128)} slice(f32[2,80,512]{2,1,0:T(8,128)} %reduce-scatter.2.cloned.1.call-done), slice={[0:2], [0:16], [0:512]} | slice | bytes 131072 | tf_op jit(solution)/shard_map/slice | solution.py:51
  78.4 35.4 %all-reduce.2.cloned.1.call-done = f32[2,64,512]{2,1,0:T(8,128)} async-done(((f32[2,64,512]{2,1,0:T(8,128)}), f32[2,64,512]{2,1,0:T(8,128)}) %all-reduce.2.cloned.1.call-update) | async-done | bytes 262160 | tf_op jit(solution)/shard_map/psum | solution.py:52
  113.8 1.7 %neg.11 = f32[2,64,512]{2,1,0:T(8,128)} negate(f32[2,64,512]{2,1,0:T(8,128)} %all-reduce.2.cloned.1.call-done) | non-fusion elementwise | flops 65536 | bytes 524288 | tf_op jit(solution)/shard_map/neg | solution.py:52
  (4 shorter events, 0.1 us)
Async XLA Ops:
  7.2 19.4 %copy-start = (f32[128,64]{0,1:T(8,128)S(1)}, f32[128,64]{0,1:T(8,128)}, u32[]{:S(2)}) copy-start(f32[128,64]{0,1:T(8,128)} %param.3) | copy-start | bytes 98308
  7.2 68.1 %reduce-scatter.2.cloned.1.call-start = ((), (), s32[]{:S(2)}) async-start(), calls=%async_computation.1 | async-start | bytes 2949120 | tf_op jit(solution)/shard_map/reduce_scatter | solution.py:50
  29.9 84.0 %all-reduce.2.cloned.1.call-start = ((), (), s32[]{:S(2)}) async-start(), calls=%async_computation.2 | async-start | bytes 524288 | tf_op jit(solution)/shard_map/psum | solution.py:52
Sparse Core Ops, SparseCore 0:
  30.0 45.2 reduce-scatter.1
  78.2 35.5 all-reduce.1
